TPU v7x, 32 devices: a whole 2x2x4 slice. The times are simulated.
32 devices in a mesh: blk: 2 (over x), head: 4 (over z), weight: 4 (over y, core).
Axes of the slice: x: 2, y: 2, z: 4, core: 2. Of those that a mesh axis runs over, the one named last changes fastest.
Arguments:
- hidden_in: bfloat16 [2048, 2, 768], P(('blk', 'head', 'weight')), may hold values from -6 to 6
- qkv_weight: bfloat16 [768, 2304], replicated, may hold values from -0.21875 to 0.21875
- query_bias: float32 [768], replicated, may hold values from -3 to 3
- value_bias: float32 [768], replicated, may hold values from -0.12 to 0.12
- out_weight: bfloat16 [768, 768], replicated, may hold values from -5.75 to 5.75
- out_bias: float32 [768], replicated, may hold values from -3 to 3
- norm1_gain: float32 [768], replicated, may hold values from 0.25 to 1.75
- norm1_bias: float32 [768], replicated, may hold values from -3 to 3
- up_weight: bfloat16 [768, 3072], P(None, 'weight'), may hold values from -0.21875 to 0.21875
- up_bias: float32 [3072], P('weight'), may hold values from -3 to 3
- down_weight: bfloat16 [3072, 768], P('weight'), may hold values from -0.109375 to 0.109375
- down_bias: float32 [768], replicated, may hold values from -3 to 3
- norm2_gain: float32 [768], replicated, may hold values from 0.25 to 1.75
- norm2_bias: float32 [768], replicated, may hold values from -3 to 3
- lengths: int32 [2], replicated, may hold values from 256 to 2048, as said below
- out_cotangent: bfloat16 [2048, 2, 768], P(('blk', 'head', 'weight')), may hold values from -6 to 6
Outputs:
- layer_out: bfloat16 [2048, 2, 768], P(('blk', 'head', 'weight'))
- grad_in: float32 [2048, 2, 768], P(('blk', 'head', 'weight'))
- grad_qkv_weight: float32 [768, 2304], replicated
- grad_query_bias: float32 [768], replicated
- grad_value_bias: float32 [768], replicated
- grad_out_weight: float32 [768, 768], replicated
- grad_out_bias: float32 [768], replicated
- grad_norm1_gain: float32 [768], replicated
- grad_norm1_bias: float32 [768], replicated
- grad_up_weight: float32 [768, 3072], P(None, 'weight')
- grad_up_bias: float32 [3072], P('weight')
- grad_down_weight: float32 [3072, 768], P('weight')
- grad_down_bias: float32 [768], replicated
- grad_norm2_gain: float32 [768], replicated
- grad_norm2_bias: float32 [768], replicated
Inputs may be any that keep to these rules, and one draw needn't show every extreme that they name: Positions 0 to lengths[b] - 1 of sequence b are tokens and the rest padding; at least one sequence has no padding.
All inputs are finite; a program needn't handle non-finite values.
Results may differ from a plain program's by a relative error of at most 0.02.
Values may be sent and summed in bfloat16 or wider, within the bound.
No kernel may reach another device: no remote copies, remote signals or barrier semaphores. Data moves between devices by JAX's collectives and lax.ppermute only.
A program may use at most 128 MiB of HBM per device.

v0:
```python
import jax
import jax.numpy as jnp
from jax import lax
from jax.sharding import PartitionSpec as P

HEADS = 12
HEAD_DIM = 64
EPS = 1e-05
SQRT_HALF = 0.7071067811865476
INV_ROOT_TAU = 0.3989422804014327


def norm_forward(resid, gain, bias):
    centre = jnp.mean(resid, axis=-1, keepdims=True)
    centred = resid - centre
    spread = jnp.mean(centred * centred, axis=-1, keepdims=True)
    rstd = lax.rsqrt(spread + EPS)
    normed = centred * rstd
    return (normed * gain + bias, normed, rstd)


def norm_backward(grad, normed, rstd, gain):
    scaled = grad * gain
    inner = (
        scaled
        - jnp.mean(scaled, axis=-1, keepdims=True)
        - normed * jnp.mean(scaled * normed, axis=-1, keepdims=True)
    )
    return (rstd * inner, jnp.sum(grad * normed, axis=0), jnp.sum(grad, axis=0))


def gelu_value(pre):
    return 0.5 * pre * (1.0 + jax.scipy.special.erf(pre * SQRT_HALF))


def gelu_slope(pre):
    return (
        0.5 * (1.0 + jax.scipy.special.erf(pre * SQRT_HALF))
        + pre * jnp.exp(-0.5 * pre * pre) * INV_ROOT_TAU
    )


def sweep(step, carry, piece):
    count = jax.tree.leaves(piece)[0].shape[0]
    size = 1024

    def advance(index, state):
        part = jax.tree.map(
            lambda leaf: lax.dynamic_slice_in_dim(leaf, index * size, size, 0), piece
        )
        return step(state, part, index * size)

    return lax.fori_loop(0, count // size, advance, carry)


def per_device(
    hidden_in,
    qkv_weight,
    query_bias,
    value_bias,
    out_weight,
    out_bias,
    norm1_gain,
    norm1_bias,
    up_weight,
    up_bias,
    down_weight,
    down_bias,
    norm2_gain,
    norm2_bias,
    lengths,
    out_cotangent,
):
    rows_here, seq_count, width = hidden_in.shape
    head_devs = lax.axis_size("head")
    weight_devs = lax.axis_size("weight")
    group = width // head_devs
    local_heads = HEADS // head_devs
    scale = HEAD_DIM ** (-0.5)
    tokens = rows_here * seq_count
    flat = hidden_in.reshape(tokens, width)
    bias_all = jnp.concatenate([query_bias, jnp.zeros((width,), jnp.float32), value_bias])
    packed = (jnp.dot(flat, qkv_weight, preferred_element_type=jnp.float32) + bias_all).astype(
        jnp.bfloat16
    )
    packed = packed.reshape(rows_here, seq_count, 3, width)
    regrouped = lax.all_to_all(packed, "head", split_axis=3, concat_axis=0, tiled=True)
    query_rows = regrouped.shape[0]
    query = regrouped[:, :, 0].reshape(query_rows, seq_count, local_heads, HEAD_DIM)
    keyval = regrouped[:, :, 1:]
    key_total = query_rows * lax.axis_size("blk") * weight_devs

    def positions(start, count):
        index = jnp.arange(count, dtype=jnp.int32) + start
        device = index // query_rows
        within = index % query_rows
        source = device // weight_devs * head_devs + within // rows_here
        return (source * weight_devs + device % weight_devs) * rows_here + within % rows_here

    def split_block(block, start):
        count = block.shape[0]
        keys = block[:, :, 0].reshape(count, seq_count, local_heads, HEAD_DIM)
        values = block[:, :, 1].reshape(count, seq_count, local_heads, HEAD_DIM)
        valid = positions(start, count)[None, :] < lengths[:, None]
        scores = (
            jnp.einsum("qbhe,kbhe->bhqk", query, keys, preferred_element_type=jnp.float32) * scale
        )
        weights = jnp.where(valid[:, None, None, :], jnp.exp(scores), 0.0)
        return (keys, values, weights)

    def forward_block(carry, block, start):
        numer, denom = carry
        keys, values, weights = split_block(block, start)
        numer = numer + jnp.einsum(
            "bhqk,kbhe->qbhe",
            weights.astype(jnp.bfloat16),
            values,
            preferred_element_type=jnp.float32,
        )
        return (numer, denom + jnp.sum(weights, axis=-1))

    first = (
        jnp.zeros((query_rows, seq_count, local_heads, HEAD_DIM), jnp.float32),
        jnp.zeros((seq_count, local_heads, query_rows), jnp.float32),
    )
    numer, denom = sweep(
        forward_block, first, lax.all_gather(keyval, ("blk", "weight"), axis=0, tiled=True)
    )
    attended = (numer / jnp.transpose(denom, (2, 0, 1))[..., None]).astype(jnp.bfloat16)
    returned = lax.all_to_all(
        attended.reshape(query_rows, seq_count, group),
        "head",
        split_axis=0,
        concat_axis=2,
        tiled=True,
    )
    attn_flat = returned.reshape(tokens, width)
    resid1 = (
        flat.astype(jnp.float32)
        + jnp.dot(attn_flat, out_weight, preferred_element_type=jnp.float32)
        + out_bias
    )
    hidden1, normed1, rstd1 = norm_forward(resid1, norm1_gain, norm1_bias)
    hidden_half = hidden1.astype(jnp.bfloat16).reshape(rows_here, seq_count, width)
    gathered = lax.all_gather(hidden_half, "weight", axis=0, tiled=True)
    gathered_flat = gathered.reshape(weight_devs * tokens, width)
    pre = jnp.dot(gathered_flat, up_weight, preferred_element_type=jnp.float32) + up_bias
    active = gelu_value(pre).astype(jnp.bfloat16)
    active_rows = active.reshape(weight_devs * rows_here, seq_count, -1)
    count = lax.axis_size("weight") * rows_here
    part = active_rows
    mixed = (
        lax.psum_scatter(
            jnp.dot(
                part.reshape(count * seq_count, -1), down_weight, preferred_element_type=jnp.float32
            )
            .reshape(count, seq_count, width)
            .astype(jnp.bfloat16),
            "weight",
            scatter_dimension=0,
            tiled=True,
        )
        .astype(jnp.float32)
        .reshape(tokens, width)
    )
    resid2 = hidden1 + mixed + down_bias
    final, normed2, rstd2 = norm_forward(resid2, norm2_gain, norm2_bias)
    layer_out = final.astype(jnp.bfloat16).reshape(rows_here, seq_count, width)
    cotangent = out_cotangent.reshape(tokens, width).astype(jnp.float32)
    grad_resid2, grad_norm2_gain, grad_norm2_bias = norm_backward(
        cotangent, normed2, rstd2, norm2_gain
    )
    grad_down_bias = jnp.sum(grad_resid2, axis=0)
    grad_mixed = grad_resid2.astype(jnp.bfloat16).reshape(rows_here, seq_count, width)
    mixed_all = lax.all_gather(grad_mixed, "weight", axis=0, tiled=True).reshape(
        weight_devs * tokens, width
    )
    grad_down_weight = jnp.dot(active.T, mixed_all, preferred_element_type=jnp.float32)
    grad_pre = jnp.dot(mixed_all, down_weight.T, preferred_element_type=jnp.float32) * gelu_slope(
        pre
    )
    grad_up_bias = jnp.sum(grad_pre, axis=0)
    grad_pre_half = grad_pre.astype(jnp.bfloat16)
    grad_up_weight = jnp.dot(gathered_flat.T, grad_pre_half, preferred_element_type=jnp.float32)
    pre_rows = grad_pre_half.reshape(weight_devs * rows_here, seq_count, -1)
    count = lax.axis_size("weight") * rows_here
    part = pre_rows
    back_hidden = (
        lax.psum_scatter(
            jnp.dot(
                part.reshape(count * seq_count, -1), up_weight.T, preferred_element_type=jnp.float32
            )
            .reshape(count, seq_count, width)
            .astype(jnp.bfloat16),
            "weight",
            scatter_dimension=0,
            tiled=True,
        )
        .astype(jnp.float32)
        .reshape(tokens, width)
    )
    grad_hidden1 = grad_resid2 + back_hidden
    grad_resid1, grad_norm1_gain, grad_norm1_bias = norm_backward(
        grad_hidden1, normed1, rstd1, norm1_gain
    )
    grad_out_bias = jnp.sum(grad_resid1, axis=0)
    grad_attn_half = grad_resid1.astype(jnp.bfloat16)
    grad_out_weight = jnp.dot(attn_flat.T, grad_attn_half, preferred_element_type=jnp.float32)
    grad_attended = jnp.dot(
        grad_attn_half, out_weight.T, preferred_element_type=jnp.float32
    ).astype(jnp.bfloat16)
    heads_grad = lax.all_to_all(
        grad_attended.reshape(rows_here, seq_count, width),
        "head",
        split_axis=2,
        concat_axis=0,
        tiled=True,
    )
    heads_grad = heads_grad.reshape(query_rows, seq_count, local_heads, HEAD_DIM)
    delta = jnp.transpose(
        jnp.sum(heads_grad.astype(jnp.float32) * attended.astype(jnp.float32), axis=-1), (1, 2, 0)
    )
    own_start = lax.axis_index(("blk", "weight")) * query_rows
    own_keys = keyval[:, :, 0].reshape(query_rows, seq_count, local_heads, HEAD_DIM)
    own_values = keyval[:, :, 1].reshape(query_rows, seq_count, local_heads, HEAD_DIM)
    own_valid = positions(own_start, query_rows)[None, :] < lengths[:, None]
    delta_rows = jnp.transpose(delta, (2, 0, 1))
    denom_rows = jnp.transpose(denom, (2, 0, 1))

    def key_side(carry, pieces, start):
        key_acc, value_acc, query_sums = carry
        query_piece, grad_piece, delta_piece, denom_piece = pieces
        count = query_piece.shape[0]
        scores = (
            jnp.einsum("qbhe,kbhe->bhqk", query_piece, own_keys, preferred_element_type=jnp.float32)
            * scale
        )
        weights = jnp.where(own_valid[:, None, None, :], jnp.exp(scores), 0.0)
        probs = weights / jnp.transpose(denom_piece, (1, 2, 0))[..., None]
        grad_prob = jnp.einsum(
            "qbhe,kbhe->bhqk", grad_piece, own_values, preferred_element_type=jnp.float32
        )
        score_half = (
            probs * (grad_prob - jnp.transpose(delta_piece, (1, 2, 0))[..., None])
        ).astype(jnp.bfloat16)
        value_acc = value_acc + jnp.einsum(
            "bhqk,qbhe->kbhe",
            probs.astype(jnp.bfloat16),
            grad_piece,
            preferred_element_type=jnp.float32,
        )
        key_acc = (
            key_acc
            + jnp.einsum(
                "bhqk,qbhe->kbhe", score_half, query_piece, preferred_element_type=jnp.float32
            )
            * scale
        )
        query_part = (
            jnp.einsum("bhqk,kbhe->qbhe", score_half, own_keys, preferred_element_type=jnp.float32)
            * scale
        )
        query_sums = lax.dynamic_update_slice_in_dim(
            query_sums, query_part.reshape(count, seq_count, group), start, 0
        )
        return (key_acc, value_acc, query_sums)

    second = (
        jnp.zeros((query_rows, seq_count, local_heads, HEAD_DIM), jnp.float32),
        jnp.zeros((query_rows, seq_count, local_heads, HEAD_DIM), jnp.float32),
        jnp.zeros((key_total, seq_count, group), jnp.float32),
    )
    key_acc, value_acc, query_sums = sweep(
        key_side,
        second,
        (
            lax.all_gather(query, ("blk", "weight"), axis=0, tiled=True),
            lax.all_gather(heads_grad, ("blk", "weight"), axis=0, tiled=True),
            lax.all_gather(
                delta_rows.astype(jnp.bfloat16), ("blk", "weight"), axis=0, tiled=True
            ).astype(jnp.float32),
            lax.all_gather(
                denom_rows.astype(jnp.bfloat16), ("blk", "weight"), axis=0, tiled=True
            ).astype(jnp.float32),
        ),
    )
    query_grad = lax.psum_scatter(
        query_sums.astype(jnp.bfloat16), ("blk", "weight"), scatter_dimension=0, tiled=True
    ).astype(jnp.float32)
    key_grad = key_acc.reshape(query_rows, seq_count, group)
    value_grad = value_acc.reshape(query_rows, seq_count, group)
    stacked = jnp.stack([query_grad, key_grad, value_grad], axis=2).astype(jnp.bfloat16)
    grad_packed = lax.all_to_all(stacked, "head", split_axis=0, concat_axis=3, tiled=True).reshape(
        tokens, 3 * width
    )
    grad_qkv_weight = jnp.dot(flat.T, grad_packed, preferred_element_type=jnp.float32)
    column_sums = jnp.sum(grad_packed.astype(jnp.float32), axis=0)
    grad_in = (
        jnp.dot(grad_packed, qkv_weight.T, preferred_element_type=jnp.float32) + grad_resid1
    ).reshape(rows_here, seq_count, width)
    shared = lax.psum(
        (
            grad_qkv_weight,
            column_sums[:width],
            column_sums[2 * width :],
            grad_out_weight,
            grad_out_bias,
            grad_norm1_gain,
            grad_norm1_bias,
            grad_norm2_gain,
            grad_norm2_bias,
            grad_down_bias,
        ),
        ("blk", "head", "weight"),
    )
    hidden_sums = (
        lax.psum(grad_up_weight.astype(jnp.bfloat16), ("blk", "head")).astype(jnp.float32),
        lax.psum(grad_up_bias.astype(jnp.bfloat16), ("blk", "head")).astype(jnp.float32),
        lax.psum(grad_down_weight.astype(jnp.bfloat16), ("blk", "head")).astype(jnp.float32),
    )
    return (
        layer_out,
        grad_in,
        shared[0],
        shared[1],
        shared[2],
        shared[3],
        shared[4],
        shared[5],
        shared[6],
        hidden_sums[0],
        hidden_sums[1],
        hidden_sums[2],
        shared[9],
        shared[7],
        shared[8],
    )


def solution(mesh):
    placed = (
        P(("blk", "head", "weight"), None, None),
        P(),
        P(),
        P(),
        P(),
        P(),
        P(),
        P(),
        P(None, "weight"),
        P("weight"),
        P("weight", None),
        P(),
        P(),
        P(),
        P(),
        P(("blk", "head", "weight"), None, None),
    )
    return jax.shard_map(
        per_device,
        mesh=mesh,
        in_specs=placed,
        out_specs=(
            P(("blk", "head", "weight"), None, None),
            P(("blk", "head", "weight"), None, None),
            P(),
            P(),
            P(),
            P(),
            P(),
            P(),
            P(),
            P(None, "weight"),
            P("weight"),
            P("weight", None),
            P(),
            P(),
            P(),
        ),
        check_vma=False,
    )
```

profile of v0, /device:TPU:0, one launch (start us, length us, event | category | flops | bytes accessed | tf_op | source)
XLA Modules:
  0.0 749.1 jit_solution(972970801593629136)
XLA Ops:
  9.8 2.4 fusion.47
  14.1 4.8 copy.83
  18.9 2.7 reshape.378
  21.6 22.3 %all_to_all.63 = bf16[4,2,36864]{2,1,0:T(2,128)(2,1)} all-to-all(bf16[4,2,36864]{2,1,0:T(2,128)(2,1)} %reshape.378), channel_id=1, replica_groups=mesh['blk'=2,'head'=4,'weight'=4] {'head'}, dimensions={0} | all-to-all | bytes 1179648 | tf_op jit(solution)/shard_map/all_to_all | solution.py:87
  43.9 2.6 reshape.379
  46.6 4.8 copy.101
  54.5 2.0 fusion.66
  58.3 32.0 %all-gather.4.cloned.1.call-done = bf16[2048,2,2,192]{3,0,2,1:T(8,128)(2,1)} async-done(((bf16[256,2,2,192]{3,0,2,1:T(8,128)(2,1)}), bf16[2048,2,2,192]{3,0,2,1:T(8,128)(2,1)}) %all-gather.4.cloned.1.call-update) | async-done | bytes 3145744 | tf_op jit(solution)/shard_map/all_gather | solution.py:127
  90.3 6.1 copy.87
  96.4 23.1 %while.37 = (s32[]{:T(128)}, f32[256,2,3,64]{0,3,2,1:T(8,128)}, f32[2,3,256]{2,1,0:T(4,128)S(1)}, bf16[2048,2,2,192]{0,3,1,2:T(8,128)(2,1)}, s32[2]{0:T(128)}, /...) while((s32[]{:T(128)}, f32[256,2,3,64]{0,3,2,1:T(8,128)}, ...), condition=%wide.region_2.3_spmd.clone, body=%wide.region_0.2_spmd.clone.sunk | while | flops 412356096 | bytes 19118340 | solution.py:53
  96.4 2.4 constant_dynamic-slice_fusion.3
  99.6 3.5 bitcast_reduce_fusion.2
  103.1 4.8 fusion.121
  107.9 2.4 constant_dynamic-slice_fusion.3
  111.1 3.5 bitcast_reduce_fusion.2
  114.6 4.9 fusion.121
  123.0 13.9 %all_to_all.64 = bf16[256,2,192]{2,1,0:T(2,128)(2,1)S(1)} all-to-all(bf16[256,2,192]{2,1,0:T(2,128)(2,1)} %copy.88), channel_id=1, replica_groups=mesh['blk'=2,'head'=4,'weight'=4] {'head'}, dimensions={0} | all-to-all | bytes 393216 | tf_op jit(solution)/shard_map/all_to_all | solution.py:130
  145.3 9.5 %all_gather.22 = bf16[256,2,768]{2,1,0:T(2,128)(2,1)} all-gather(bf16[64,2,768]{2,1,0:T(2,128)(2,1)} %reshape.355), channel_id=1, replica_groups=mesh['blk'=2,'head'=4,'weight'=4] {'weight'}, dimensions={0}, use_global_device_ids=true | all-gather | bytes 983040 | tf_op jit(solution)/shard_map/all_gather | solution.py:145
  154.8 3.0 reshape.356
  157.7 3.6 multiply_convert_fusion.1
  163.9 2.9 convert_element_type.130
  174.6 26.6 %all-reduce.10.cloned.1.call-done = bf16[256,2,768]{2,1,0:T(2,128)(2,1)} async-done(((bf16[256,2,768]{2,1,0:T(2,128)(2,1)}), bf16[256,2,768]{2,1,0:T(2,128)(2,1)}) %all-reduce.10.cloned.1.call-update) | async-done | bytes 786448
  203.0 2.0 reshape.369
  212.0 9.3 %all_gather.25 = bf16[256,2,768]{2,1,0:T(2,128)(2,1)} all-gather(bf16[64,2,768]{2,1,0:T(2,128)(2,1)} %reshape.360), channel_id=1, replica_groups=mesh['blk'=2,'head'=4,'weight'=4] {'weight'}, dimensions={0}, use_global_device_ids=true | all-gather | bytes 983040 | tf_op jit(solution)/shard_map/all_gather | solution.py:175
  221.3 3.0 reshape.361
  224.3 3.8 fusion.69
  230.7 2.8 convert_element_type.140
  234.2 35.0 %all-reduce.12.cloned.1.call-done = bf16[256,2,768]{2,1,0:T(2,128)(2,1)} async-done(((bf16[256,2,768]{2,1,0:T(2,128)(2,1)}), bf16[256,2,768]{2,1,0:T(2,128)(2,1)}) %all-reduce.12.cloned.1.call-update) | async-done | bytes 786448
  271.0 2.0 reshape.372
  273.0 2.2 multiply_reduce_fusion.1
  280.3 2.0 copy.92
  282.3 2.0 reshape.380
  284.3 11.5 %all_to_all.65 = bf16[4,2,12288]{2,1,0:T(2,128)(2,1)} all-to-all(bf16[4,2,12288]{2,1,0:T(2,128)(2,1)} %reshape.380), channel_id=1, replica_groups=mesh['blk'=2,'head'=4,'weight'=4] {'head'}, dimensions={0} | all-to-all | bytes 393216 | tf_op jit(solution)/shard_map/all_to_all | solution.py:212
  297.8 2.0 copy.105
  299.8 2.0 reshape.365
  305.5 8.9 %all_gather.24 = bf16[2048,2,3]{0,2,1:T(4,128)(2,1)S(1)} all-gather(bf16[256,2,3]{0,2,1:T(4,128)(2,1)S(1)} %bitcast_convert_fusion.6), channel_id=1, replica_groups=mesh['blk'=2,'head'=4,'weight'=4] {'blk','weight'}, dimensions={0}, use_global_device_ids=true | all-gather | bytes 27648 | tf_op jit(solution)/shard_map/all_gather | solution.py:282
  316.2 8.6 %all_gather.27 = bf16[2048,2,3]{0,2,1:T(4,128)(2,1)S(1)} all-gather(bf16[256,2,3]{0,2,1:T(4,128)(2,1)S(1)} %multiply_reduce_fusion.2), channel_id=1, replica_groups=mesh['blk'=2,'head'=4,'weight'=4] {'blk','weight'}, dimensions={0}, use_global_device_ids=true | all-gather | bytes 27648 | tf_op jit(solution)/shard_map/all_gather | solution.py:279
  327.4 38.4 %while.38 = (s32[]{:T(128)}, f32[256,2,3,64]{0,3,2,1:T(8,128)}, f32[256,2,3,64]{0,3,2,1:T(8,128)}, bf16[2048,2,192]{0,2,1:T(8,128)(2,1)}, bf16[2048,2,3,64]{0,3,...) while((s32[]{:T(128)}, f32[256,2,3,64]{0,3,2,1:T(8,128)}, ...), condition=%wide.region_15.16_spmd.clone, body=%wide.region_14.15_spmd.clone.sunk | while | flops 1018921472 | bytes 103770656 | solution.py:53
  329.0 3.7 select_divide_fusion.2
  332.7 3.3 multiply_convert_fusion.3
  336.4 3.7 fusion.132
  340.1 3.7 fusion.133
  348.1 3.7 select_divide_fusion.2
  351.9 3.3 multiply_convert_fusion.3
  355.5 3.8 fusion.132
  359.3 3.7 fusion.133
  365.9 3.3 convolution_convert_fusion.1
  374.6 29.7 %reduce-scatter.2.cloned.1.call-done = bf16[256,2,192]{0,2,1:T(8,128)(2,1)} async-done(((bf16[2048,2,192]{0,2,1:T(8,128)(2,1)}), bf16[256,2,192]{0,2,1:T(8,128)(2,1)}) %reduce-scatter.2.cloned.1.call-update) | async-done | bytes 196624 | tf_op jit(solution)/shard_map/reduce_scatter | solution.py:287
  404.3 2.0 pad_maximum_fusion
  406.3 3.0 copy.96
  409.3 4.6 all-to-all-start.3
  413.9 3.0 fusion.57
  416.9 37.5 %all-to-all-done.3 = bf16[256,2,3,192]{3,1,2,0:T(2,128)(2,1)} async-done(((bf16[256,2,3,192]{3,1,2,0:T(2,128)(2,1)}), bf16[256,2,3,192]{3,1,2,0:T(2,128)(2,1)}, u32[]{:S(2)}, u32[]{:S(2)}) %all-to-all-start.3) | async-done | bytes 589856 | tf_op jit(solution)/shard_map/all_to_all | solution.py:293
  458.1 2.6 reshape.366
  460.7 5.2 convolution_bitcast_fusion
  467.6 19.1 %psum.99 = bf16[768]{0:T(1024)(128)(2,1)S(1)} all-reduce(bf16[768]{0:T(1024)(128)(2,1)S(1)} %copy-done.35), channel_id=1, replica_groups=mesh['blk'=2,'head'=4,'weight'=4] {'blk','head'}, use_global_device_ids=true, to_apply=%region_30.31 | all-reduce | flops 768 | bytes 3072 | tf_op jit(solution)/shard_map/psum | solution.py:318
  487.3 45.9 %all-reduce.16.cloned.1.call-done = (bf16[768,768]{1,0:T(8,128)(2,1)}, bf16[768,768]{1,0:T(8,128)(2,1)}) async-done(((bf16[768,768]{1,0:T(8,128)(2,1)}, bf16[768,768]{1,0:T(8,128)(2,1)}), (bf16[768,768]{1,0:T(8,128)(2,1)}, bf16[768,768]{1,0:T(8,128)(2,1)})) %all-reduce.16.cloned.1.call-update) | async-done | bytes 2359312 | tf_op jit(solution)/shard_map/psum | solution.py:317
  533.3 2.9 convert_element_type.150
  537.8 2.0 convolution_add_fusion.3
  539.8 2.0 reshape.367
  546.5 42.4 %all-reduce.2 = (f32[768]{0:T(1024)}, f32[768]{0:T(1024)}, f32[768]{0:T(1024)}, f32[768]{0:T(1024)}, f32[768]{0:T(1024)}, /*index=5*/f32[768]{0:T(1024)}, f32[768]{0:T(1024)}, f32[768]{0:T(1024)}) all-reduce(f32[768]{0:T(1024)} %slice.53, f32[768]{0:T(1024)} %slice.55, ...), channel_id=1, replica_groups=mesh['blk'=2,'head'=4,'weight'=4] {'blk','head','weight'}, use_global_device_ids=true, to_apply=%region_19.20 | all-reduce | flops 6144 | bytes 49152 | tf_op jit(solution)/shard_map/psum | solution.py:301
  588.9 142.2 %all-reduce.14.cloned.1.call-done = (f32[768,2304]{0,1:T(8,128)}, f32[768,768]{1,0:T(8,128)}) async-done(((f32[768,2304]{0,1:T(8,128)}, f32[768,768]{1,0:T(8,128)}), (f32[768,2304]{0,1:T(8,128)}, f32[768,768]{1,0:T(8,128)})) %all-reduce.14.cloned.1.call-update) | async-done | bytes 9437200 | tf_op jit(solution)/shard_map/psum | solution.py:301
  731.1 8.0 %copy.99 = f32[768,2304]{1,0:T(8,128)} copy(f32[768,2304]{0,1:T(8,128)} %get-tuple-element.630) | data formatting | bytes 14155776
  739.1 3.2 copy.134
  (205 shorter events, 88.1 us)
Async XLA Ops:
  7.2 2.6 copy-start
  7.2 83.1 %all-gather.4.cloned.1.call-start = ((), (), s32[]{:S(2)}) async-start(), calls=%async_computation.5 | async-start | bytes 4718592 | tf_op jit(solution)/shard_map/all_gather | solution.py:127
  52.7 0.9 copy-start.17
  54.4 146.7 %all-reduce.10.cloned.1.call-start = ((), (), s32[]{:S(2)}) async-start(), calls=%async_computation.9 | async-start | bytes 1572864
  96.4 3.2 copy-start.22
  99.6 3.5 copy-start.24
  107.9 3.2 copy-start.22
  111.1 3.5 copy-start.24
  136.9 5.9 copy-start.25
  136.9 5.9 copy-start.27
  141.5 0.8 copy-start.7
  141.5 0.7 copy-start.31
  142.3 0.5 copy-start.32
  143.6 14.1 %copy-start.38 = (f32[768]{0:T(1024)S(1)}, f32[768]{0:T(1024)}, u32[]{:S(2)}) copy-start(f32[768]{0:T(1024)} %param.29) | copy-start | bytes 9220
  157.7 4.5 copy-start.36
  161.4 0.9 copy-start.39
  163.9 4.9 copy-start.26
  166.8 102.4 %all-reduce.12.cloned.1.call-start = ((), (), s32[]{:S(2)}) async-start(), calls=%async_computation.10 | async-start | bytes 1572864
  205.0 1.7 copy-start.20
  205.0 2.4 copy-start.33
  205.0 2.4 copy-start.34
  208.9 0.7 copy-start.19
  224.3 4.7 copy-start.37
  228.0 1.0 copy-start.41
  233.6 91.8 %all-gather.6.cloned.1.call-start = ((), (), s32[]{:S(2)}) async-start(), calls=%async_computation.6 | async-start | bytes 1769472 | tf_op jit(solution)/shard_map/all_gather | solution.py:277
  234.1 92.0 %all-gather.8.cloned.1.call-start = ((), (), s32[]{:S(2)}) async-start(), calls=%async_computation.7 | async-start | bytes 1769472 | tf_op jit(solution)/shard_map/all_gather | solution.py:278
  273.0 2.2 copy-start.8
  273.0 4.4 copy-start.18
  276.7 0.7 copy-start.15
  301.9 102.4 %reduce-scatter.2.cloned.1.call-start = ((), (), s32[]{:S(2)}) async-start(), calls=%async_computation.8 | async-start | bytes 1769472 | tf_op jit(solution)/shard_map/reduce_scatter | solution.py:287
  328.9 3.8 copy-start.3
  328.9 3.8 copy-start.12
  332.7 3.7 copy-start.2
  336.3 3.7 copy-start.4
  336.4 3.7 copy-start.5
  340.1 3.8 copy-start.1
  340.1 3.8 copy-start.10
  343.8 1.1 copy-start.6
  343.8 1.5 copy-start.13
  345.5 1.1 copy-start.14
  348.1 3.8 copy-start.3
  348.1 3.8 copy-start.12
  351.9 3.7 copy-start.2
  355.5 3.8 copy-start.4
  355.5 3.8 copy-start.5
  359.3 3.8 copy-start.1
  359.3 3.8 copy-start.10
  363.0 1.1 copy-start.6
  363.1 1.5 copy-start.13
  364.7 1.1 copy-start.14
  365.9 167.4 %all-reduce.16.cloned.1.call-start = ((), (), s32[]{:S(2)}) async-start(), calls=%async_computation.12 | async-start | bytes 4718592 | tf_op jit(solution)/shard_map/psum | solution.py:317
  365.9 3.3 copy-start.23
  365.9 3.3 copy-start.40
  409.3 45.2 %all-to-all-start.3 = ((bf16[256,2,3,192]{3,1,2,0:T(2,128)(2,1)}), bf16[256,2,3,192]{3,1,2,0:T(2,128)(2,1)}, u32[]{:S(2)}, u32[]{:S(2)}) async-start(bf16[256,2,3,192]{3,1,2,0:T(2,128)(2,1)} %copy.96), calls=%async_computation.4 | async-start | bytes 1572864 | tf_op jit(solution)/shard_map/all_to_all | solution.py:293
  413.9 317.2 %all-reduce.14.cloned.1.call-start = ((), (), s32[]{:S(2)}) async-start(), calls=%async_computation.11 | async-start | bytes 18874368 | tf_op jit(solution)/shard_map/psum | solution.py:301
  455.7 0.9 copy-start.11
  465.9 1.7 copy-start.35
  533.3 2.9 copy-start.21
  536.2 1.6 copy-start.9
  536.2 1.6 copy-start.16
  539.8 6.6 copy-start.28
  539.8 6.6 copy-start.29
  539.8 6.6 copy-start.30
Sparse Core Ops, SparseCore 0:
  54.6 35.6 all-gather.3
  166.9 34.1 all-reduce.9
  233.7 35.4 all-reduce.11
  270.9 25.7 all-gather.5
  302.0 24.0 all-gather.7
  366.0 38.2 reduce-scatter.1
  408.4 124.7 all-reduce.15
  539.8 191.2 all-reduce.13
where the time goes:
time: 752 us; the launch traced here: 749 us
  waiting for transfers between devices  350 us (47%)
  blocking collectives  146 us (19%)
  local copies, waits for them, and re-layouts  118 us (16%)
  matrix products  79.5 us (11%)
  other arithmetic  35 us (5%)
  between operations  15.1 us (2%)
    psum x1, waiting for transfers between devices, per_device(): lax.psum((grad_qkv_weight, column_sums[:width], column_sums[2 * width:],...  142 us
    unnamed x10, waiting for transfers between devices  62.2 us
    psum x1, waiting for transfers between devices, per_device(): lax.psum(grad_up_weight.astype(jnp.bfloat16), ('blk', 'head'))  45.9 us
    psum x1, blocking collectives, per_device(): lax.psum((grad_qkv_weight, column_sums[:width], column_sums[2 * width:],...  42.4 us
    all_to_all x1, waiting for transfers between devices, per_device(): lax.all_to_all(stacked, 'head', split_axis=0, concat_axis=3, tiled=True)  37.5 us
    unnamed x68, local copies, waits for them, and re-layouts  34.1 us
    all_gather x1, waiting for transfers between devices, per_device(): lax.all_gather(keyval, ('blk', 'weight'), axis=0, tiled=True)  32 us
    reduce_scatter x1, waiting for transfers between devices, per_device(): lax.psum_scatter(query_sums.astype(jnp.bfloat16), ('blk', 'weight'), scat...  29.7 us
  transfers between devices with their start and end apart: 9, of which 8 were waited for; matrix products, arithmetic and copies ran while one was open for 11% of the time, Pallas kernels for 0%

commit v1 on v0

--- a/solution.py
+++ b/solution.py
@@ -314,7 +314,9 @@
         ("blk", "head", "weight"),
     )
     hidden_sums = (
-        lax.psum(grad_up_weight.astype(jnp.bfloat16), ("blk", "head")).astype(jnp.float32),
+        jnp.sum(
+            lax.all_gather(grad_up_weight.astype(jnp.bfloat16), ("blk", "head")), axis=0
+        ).astype(jnp.float32),
         lax.psum(grad_up_bias.astype(jnp.bfloat16), ("blk", "head")).astype(jnp.float32),
         lax.psum(grad_down_weight.astype(jnp.bfloat16), ("blk", "head")).astype(jnp.float32),
     )

time: 752 us -> 865 us (1.15)
  waiting for transfers between devices: 350 us -> 455 us
    all_gather x0 -> x1, waiting for transfers between devices: none -> 132 us  [per_device(): lax.all_gather(grad_up_weight.astype(jnp.bfloat16), ('blk', 'head'))]
    psum x1, waiting for transfers between devices: 45.9 us -> 24.9 us  [per_device(): lax.psum(grad_down_weight.astype(jnp.bfloat16), ('blk', 'head'))]
    all_to_all x1, waiting for transfers between devices: 37.5 us -> 24.4 us  [per_device(): lax.all_to_all(stacked, 'head', split_axis=0, concat_axis=3, tiled=True)]
    unnamed x68 -> x64, local copies, waits for them, and re-layouts: 34.1 us -> 32.2 us
    unnamed x10 -> x11, waiting for transfers between devices: 62.2 us -> 62.2 us
  transfers between devices with their start and end apart: 9 -> 10, of which waited for: 8 -> 9; matrix products, arithmetic and copies ran while one was open for 11% -> 10% of each run, Pallas kernels for 0% -> 0%
where the time goes in v1:
time: 865 us; the launch traced here: 862 us
  waiting for transfers between devices  455 us (53%)
  blocking collectives  146 us (17%)
  local copies, waits for them, and re-layouts  117 us (14%)
  matrix products  80.5 us (9%)
  other arithmetic  42.7 us (5%)
  between operations  14.8 us (2%)
    psum x1, waiting for transfers between devices, per_device(): lax.psum((grad_qkv_weight, column_sums[:width], column_sums[2 * width:],...  144 us
    all_gather x1, waiting for transfers between devices, per_device(): lax.all_gather(grad_up_weight.astype(jnp.bfloat16), ('blk', 'head'))  132 us
    unnamed x11, waiting for transfers between devices  62.2 us
    psum x1, blocking collectives, per_device(): lax.psum((grad_qkv_weight, column_sums[:width], column_sums[2 * width:],...  42.9 us
    reduce_scatter x1, waiting for transfers between devices, per_device(): lax.psum_scatter(query_sums.astype(jnp.bfloat16), ('blk', 'weight'), scat...  35 us
    unnamed x64, local copies, waits for them, and re-layouts  32.2 us
    all_gather x1, waiting for transfers between devices, per_device(): lax.all_gather(keyval, ('blk', 'weight'), axis=0, tiled=True)  32 us
    psum x1, waiting for transfers between devices, per_device(): lax.psum(grad_down_weight.astype(jnp.bfloat16), ('blk', 'head'))  24.9 us
  transfers between devices with their start and end apart: 10, of which 9 were waited for; matrix products, arithmetic and copies ran while one was open for 10% of the time, Pallas kernels for 0%

profile of v1, /device:TPU:0, one launch (start us, length us, event | category | flops | bytes accessed | tf_op | source)
XLA Modules:
  0.0 861.5 jit_solution(7300815515893598700)
XLA Ops:
  9.8 2.4 fusion.47
  14.1 4.8 copy.83
  18.9 2.7 reshape.379
  21.6 22.3 %all_to_all.63 = bf16[4,2,36864]{2,1,0:T(2,128)(2,1)} all-to-all(bf16[4,2,36864]{2,1,0:T(2,128)(2,1)} %reshape.379), channel_id=1, replica_groups=mesh['blk'=2,'head'=4,'weight'=4] {'head'}, dimensions={0} | all-to-all | bytes 1179648 | tf_op jit(solution)/shard_map/all_to_all | solution.py:87
  43.9 2.6 reshape.380
  46.6 4.8 copy.101
  54.5 2.0 fusion.66
  58.3 32.0 %all-gather.6.cloned.1.call-done = bf16[2048,2,2,192]{3,0,2,1:T(8,128)(2,1)} async-done(((bf16[256,2,2,192]{3,0,2,1:T(8,128)(2,1)}), bf16[2048,2,2,192]{3,0,2,1:T(8,128)(2,1)}) %all-gather.6.cloned.1.call-update) | async-done | bytes 3145744 | tf_op jit(solution)/shard_map/all_gather | solution.py:127
  90.3 6.1 copy.87
  96.4 23.2 %while.37 = (s32[]{:T(128)}, f32[256,2,3,64]{0,3,2,1:T(8,128)}, f32[2,3,256]{2,1,0:T(4,128)S(1)}, bf16[2048,2,2,192]{0,3,1,2:T(8,128)(2,1)}, s32[2]{0:T(128)}, /...) while((s32[]{:T(128)}, f32[256,2,3,64]{0,3,2,1:T(8,128)}, ...), condition=%wide.region_2.3_spmd.clone, body=%wide.region_0.2_spmd.clone.sunk | while | flops 412356096 | bytes 19118340 | solution.py:53
  96.4 2.4 constant_dynamic-slice_fusion.3
  99.6 3.5 bitcast_reduce_fusion.2
  103.1 4.8 fusion.121
  107.9 2.4 constant_dynamic-slice_fusion.3
  111.1 3.5 bitcast_reduce_fusion.2
  114.6 4.9 fusion.121
  123.1 13.9 %all_to_all.64 = bf16[256,2,192]{2,1,0:T(2,128)(2,1)S(1)} all-to-all(bf16[256,2,192]{2,1,0:T(2,128)(2,1)} %copy.88), channel_id=1, replica_groups=mesh['blk'=2,'head'=4,'weight'=4] {'head'}, dimensions={0} | all-to-all | bytes 393216 | tf_op jit(solution)/shard_map/all_to_all | solution.py:130
  145.3 9.5 %all_gather.28 = bf16[256,2,768]{2,1,0:T(2,128)(2,1)} all-gather(bf16[64,2,768]{2,1,0:T(2,128)(2,1)} %reshape.355), channel_id=1, replica_groups=mesh['blk'=2,'head'=4,'weight'=4] {'weight'}, dimensions={0}, use_global_device_ids=true | all-gather | bytes 983040 | tf_op jit(solution)/shard_map/all_gather | solution.py:145
  154.8 3.0 reshape.356
  157.8 3.6 multiply_convert_fusion.1
  164.0 2.9 convert_element_type.132
  174.7 26.6 %all-reduce.11.cloned.1.call-done = bf16[256,2,768]{2,1,0:T(2,128)(2,1)} async-done(((bf16[256,2,768]{2,1,0:T(2,128)(2,1)}), bf16[256,2,768]{2,1,0:T(2,128)(2,1)}) %all-reduce.11.cloned.1.call-update) | async-done | bytes 786448
  203.1 2.0 reshape.369
  212.2 9.3 %all_gather.31 = bf16[256,2,768]{2,1,0:T(2,128)(2,1)} all-gather(bf16[64,2,768]{2,1,0:T(2,128)(2,1)} %reshape.360), channel_id=1, replica_groups=mesh['blk'=2,'head'=4,'weight'=4] {'weight'}, dimensions={0}, use_global_device_ids=true | all-gather | bytes 983040 | tf_op jit(solution)/shard_map/all_gather | solution.py:175
  221.5 3.0 reshape.361
  224.4 3.8 fusion.69
  230.8 2.8 convert_element_type.142
  234.2 35.0 %all-reduce.13.cloned.1.call-done = bf16[256,2,768]{2,1,0:T(2,128)(2,1)} async-done(((bf16[256,2,768]{2,1,0:T(2,128)(2,1)}), bf16[256,2,768]{2,1,0:T(2,128)(2,1)}) %all-reduce.13.cloned.1.call-update) | async-done | bytes 786448
  271.1 2.0 reshape.372
  273.1 2.2 multiply_reduce_fusion.1
  280.4 2.0 copy.92
  284.4 11.5 %all_to_all.65 = bf16[4,2,12288]{2,1,0:T(2,128)(2,1)} all-to-all(bf16[4,2,12288]{2,1,0:T(2,128)(2,1)} %reshape.381), channel_id=1, replica_groups=mesh['blk'=2,'head'=4,'weight'=4] {'head'}, dimensions={0} | all-to-all | bytes 393216 | tf_op jit(solution)/shard_map/all_to_all | solution.py:212
  297.9 2.0 copy.105
  305.6 8.8 %all_gather.30 = bf16[2048,2,3]{0,2,1:T(4,128)(2,1)S(1)} all-gather(bf16[256,2,3]{0,2,1:T(4,128)(2,1)S(1)} %bitcast_convert_fusion.6), channel_id=1, replica_groups=mesh['blk'=2,'head'=4,'weight'=4] {'blk','weight'}, dimensions={0}, use_global_device_ids=true | all-gather | bytes 27648 | tf_op jit(solution)/shard_map/all_gather | solution.py:282
  316.2 8.6 %all_gather.33 = bf16[2048,2,3]{0,2,1:T(4,128)(2,1)S(1)} all-gather(bf16[256,2,3]{0,2,1:T(4,128)(2,1)S(1)} %multiply_reduce_fusion.2), channel_id=1, replica_groups=mesh['blk'=2,'head'=4,'weight'=4] {'blk','weight'}, dimensions={0}, use_global_device_ids=true | all-gather | bytes 27648 | tf_op jit(solution)/shard_map/all_gather | solution.py:279
  327.5 38.3 %while.38 = (s32[]{:T(128)}, f32[256,2,3,64]{0,3,2,1:T(8,128)}, f32[256,2,3,64]{0,3,2,1:T(8,128)}, bf16[2048,2,192]{0,2,1:T(8,128)(2,1)}, bf16[2048,2,3,64]{0,3,...) while((s32[]{:T(128)}, f32[256,2,3,64]{0,3,2,1:T(8,128)}, ...), condition=%wide.region_15.16_spmd.clone, body=%wide.region_14.15_spmd.clone.sunk | while | flops 1018921472 | bytes 103770656 | solution.py:53
  329.0 3.7 select_divide_fusion.2
  332.8 3.3 multiply_convert_fusion.3
  336.4 3.7 fusion.132
  340.1 3.7 fusion.133
  348.1 3.7 select_divide_fusion.2
  351.9 3.3 multiply_convert_fusion.3
  355.5 3.7 fusion.132
  359.3 3.7 fusion.133
  369.2 35.0 %reduce-scatter.2.cloned.1.call-done = bf16[256,2,192]{0,2,1:T(8,128)(2,1)} async-done(((bf16[2048,2,192]{0,2,1:T(8,128)(2,1)}), bf16[256,2,192]{0,2,1:T(8,128)(2,1)}) %reduce-scatter.2.cloned.1.call-update) | async-done | bytes 196624 | tf_op jit(solution)/shard_map/reduce_scatter | solution.py:287
  406.2 3.0 copy.96
  409.2 4.6 all-to-all-start.3
  413.8 3.2 convolution_convert_fusion
  417.1 3.0 fusion.57
  420.1 24.4 %all-to-all-done.3 = bf16[256,2,3,192]{3,1,2,0:T(2,128)(2,1)} async-done(((bf16[256,2,3,192]{3,1,2,0:T(2,128)(2,1)}), bf16[256,2,3,192]{3,1,2,0:T(2,128)(2,1)}, u32[]{:S(2)}, u32[]{:S(2)}) %all-to-all-start.3) | async-done | bytes 589856 | tf_op jit(solution)/shard_map/all_to_all | solution.py:293
  448.2 2.7 reshape.366
  450.8 5.2 convolution_bitcast_fusion
  456.1 3.2 convolution_convert_fusion.1
  461.0 19.4 %psum.91 = bf16[768]{0:T(1024)(128)(2,1)S(1)} all-reduce(bf16[768]{0:T(1024)(128)(2,1)S(1)} %copy-done.34), channel_id=1, replica_groups=mesh['blk'=2,'head'=4,'weight'=4] {'blk','head'}, use_global_device_ids=true, to_apply=%region_30.31 | all-reduce | flops 768 | bytes 3072 | tf_op jit(solution)/shard_map/psum | solution.py:320
  481.0 24.9 %all-reduce.9.cloned.1.call-done = bf16[768,768]{1,0:T(8,128)(2,1)} async-done(((bf16[768,768]{1,0:T(8,128)(2,1)}), bf16[768,768]{1,0:T(8,128)(2,1)}) %all-reduce.9.cloned.1.call-update) | async-done | bytes 1179664 | tf_op jit(solution)/shard_map/psum | solution.py:321
  505.9 2.9 convert_element_type.156
  508.8 2.0 convolution_add_fusion.3
  510.9 2.0 reshape.367
  517.5 42.9 %all-reduce.2 = (f32[768]{0:T(1024)}, f32[768]{0:T(1024)}, f32[768]{0:T(1024)}, f32[768]{0:T(1024)}, f32[768]{0:T(1024)}, /*index=5*/f32[768]{0:T(1024)}, f32[768]{0:T(1024)}, f32[768]{0:T(1024)}) all-reduce(f32[768]{0:T(1024)} %slice.53, f32[768]{0:T(1024)} %slice.55, ...), channel_id=1, replica_groups=mesh['blk'=2,'head'=4,'weight'=4] {'blk','head','weight'}, use_global_device_ids=true, to_apply=%region_19.20 | all-reduce | flops 6144 | bytes 49152 | tf_op jit(solution)/shard_map/psum | solution.py:301
  560.4 143.9 %all-reduce.15.cloned.1.call-done = (f32[768,2304]{0,1:T(8,128)}, f32[768,768]{1,0:T(8,128)}) async-done(((f32[768,2304]{0,1:T(8,128)}, f32[768,768]{1,0:T(8,128)}), (f32[768,2304]{0,1:T(8,128)}, f32[768,768]{1,0:T(8,128)})) %all-reduce.15.cloned.1.call-update) | async-done | bytes 9437200 | tf_op jit(solution)/shard_map/psum | solution.py:301
  704.3 8.0 copy.99
  712.3 132.0 %all-gather.12.cloned.1.call-done = bf16[6144,768]{1,0:T(8,128)(2,1)} async-done(((bf16[768,768]{1,0:T(8,128)(2,1)}), bf16[6144,768]{1,0:T(8,128)(2,1)}) %all-gather.12.cloned.1.call-update) | async-done | bytes 9437200 | tf_op jit(solution)/shard_map/all_gather | solution.py:318
  844.3 6.3 reduce_sum.195
  850.6 3.0 convert_element_type.152
  (205 shorter events, 92.1 us)
Async XLA Ops:
  7.2 2.6 copy-start
  7.2 83.1 %all-gather.6.cloned.1.call-start = ((), (), s32[]{:S(2)}) async-start(), calls=%async_computation.5 | async-start | bytes 4718592 | tf_op jit(solution)/shard_map/all_gather | solution.py:127
  52.7 0.9 copy-start.17
  54.4 146.8 %all-reduce.11.cloned.1.call-start = ((), (), s32[]{:S(2)}) async-start(), calls=%async_computation.11 | async-start | bytes 1572864
  96.4 3.2 copy-start.22
  99.5 3.5 copy-start.23
  107.9 3.2 copy-start.22
  111.1 3.5 copy-start.23
  137.0 5.8 copy-start.24
  137.0 5.8 copy-start.26
  141.6 0.8 copy-start.7
  141.6 0.7 copy-start.30
  142.3 0.5 copy-start.31
  143.6 14.1 %copy-start.37 = (f32[768]{0:T(1024)S(1)}, f32[768]{0:T(1024)}, u32[]{:S(2)}) copy-start(f32[768]{0:T(1024)} %param.29) | copy-start | bytes 9220
  157.8 4.6 copy-start.35
  161.4 1.0 copy-start.38
  164.0 4.9 copy-start.25
  166.9 102.3 %all-reduce.13.cloned.1.call-start = ((), (), s32[]{:S(2)}) async-start(), calls=%async_computation.12 | async-start | bytes 1572864
  205.1 1.7 copy-start.20
  205.1 2.4 copy-start.32
  205.1 2.4 copy-start.33
  209.0 0.7 copy-start.19
  224.4 4.6 copy-start.36
  228.2 0.9 copy-start.39
  233.6 91.8 %all-gather.8.cloned.1.call-start = ((), (), s32[]{:S(2)}) async-start(), calls=%async_computation.6 | async-start | bytes 1769472 | tf_op jit(solution)/shard_map/all_gather | solution.py:277
  234.2 92.0 %all-gather.10.cloned.1.call-start = ((), (), s32[]{:S(2)}) async-start(), calls=%async_computation.7 | async-start | bytes 1769472 | tf_op jit(solution)/shard_map/all_gather | solution.py:278
  273.1 2.2 copy-start.8
  273.1 4.4 copy-start.18
  276.7 0.7 copy-start.15
  301.9 102.3 %reduce-scatter.2.cloned.1.call-start = ((), (), s32[]{:S(2)}) async-start(), calls=%async_computation.8 | async-start | bytes 1769472 | tf_op jit(solution)/shard_map/reduce_scatter | solution.py:287
  329.0 3.8 copy-start.3
  329.0 3.8 copy-start.12
  332.8 3.7 copy-start.2
  336.4 3.7 copy-start.4
  336.4 3.7 copy-start.5
  340.1 3.8 copy-start.1
  340.1 3.8 copy-start.10
  343.8 1.1 copy-start.6
  343.9 1.5 copy-start.13
  345.5 1.1 copy-start.14
  348.1 3.8 copy-start.3
  348.1 3.8 copy-start.12
  351.9 3.7 copy-start.2
  355.5 3.7 copy-start.4
  355.5 3.7 copy-start.5
  359.3 3.8 copy-start.1
  359.3 3.8 copy-start.10
  363.0 1.1 copy-start.6
  363.0 1.5 copy-start.13
  364.6 1.1 copy-start.14
  409.2 35.3 %all-to-all-start.3 = ((bf16[256,2,3,192]{3,1,2,0:T(2,128)(2,1)}), bf16[256,2,3,192]{3,1,2,0:T(2,128)(2,1)}, u32[]{:S(2)}, u32[]{:S(2)}) async-start(bf16[256,2,3,192]{3,1,2,0:T(2,128)(2,1)} %copy.96), calls=%async_computation.4 | async-start | bytes 1572864 | tf_op jit(solution)/shard_map/all_to_all | solution.py:293
  413.8 92.1 %all-reduce.9.cloned.1.call-start = ((), (), s32[]{:S(2)}) async-start(), calls=%async_computation.9 | async-start | bytes 2359296 | tf_op jit(solution)/shard_map/psum | solution.py:321
  417.0 287.3 %all-reduce.15.cloned.1.call-start = ((), (), s32[]{:S(2)}) async-start(), calls=%async_computation.13 | async-start | bytes 18874368 | tf_op jit(solution)/shard_map/psum | solution.py:301
  445.8 0.9 copy-start.11
  456.0 388.3 %all-gather.12.cloned.1.call-start = ((), (), s32[]{:S(2)}) async-start(), calls=%async_computation.10 | async-start | bytes 10616832 | tf_op jit(solution)/shard_map/all_gather | solution.py:318
  459.3 1.7 copy-start.34
  505.9 2.9 copy-start.9
  505.9 2.9 copy-start.16
  510.9 6.6 copy-start.27
  510.9 6.6 copy-start.28
  510.9 6.6 copy-start.29
  850.6 3.0 copy-start.21
Sparse Core Ops, SparseCore 0:
  54.6 35.6 all-gather.5
  167.0 34.2 all-reduce.10
  233.7 35.4 all-reduce.12
  271.0 25.7 all-gather.7
  302.0 24.0 all-gather.9
  365.9 38.2 reduce-scatter.1
  418.7 87.1 all-reduce.8
  513.0 191.2 all-reduce.14
  707.0 137.2 all-gather.11
